TPU v7x, 32 devices: a whole 2x2x4 slice. The times are simulated.
32 devices in a mesh: seq: 16 (over z, y, x), head: 2 (over core).
Axes of the slice: x: 2, y: 2, z: 4, core: 2. Of those that a mesh axis runs over, the one named last changes fastest.
Arguments:
- block_in: bfloat16 [8192, 768], P(('seq', 'head')), may hold values from -6 to 6
- grad_out: bfloat16 [8192, 768], P(('seq', 'head')), may hold values from -6 to 6
- lengths: int32 [2], replicated, may hold values from 1024 to 4096, as said below
- norm_gain: float32 [768], replicated, may hold values from 0.25 to 1.75
- w_in: bfloat16 [768, 3352], replicated, may hold values from -0.21875 to 0.21875
- conv_w: float32 [4, 1792], replicated, may hold values from -3 to 3
- conv_b: float32 [1792], replicated, may hold values from -0.5 to 0.5
- dt_bias: float32 [24], replicated, may hold values from -6 to -3.5
- a_log: float32 [24], replicated, may hold values from -10.5 to 1.4
- d_skip: float32 [24], replicated, may hold values from 0.5 to 2
- gate_gain: float32 [1536], replicated, may hold values from 0.25 to 1.75
- w_out: bfloat16 [1536, 768], replicated, may hold values from -0.15625 to 0.15625
Outputs:
- block_out: bfloat16 [8192, 768], P(('seq', 'head'))
- grad_in: float32 [8192, 768], P(('seq', 'head'))
- grad_norm_gain: float32 [768], replicated
- grad_w_in: float32 [768, 3352], replicated
- grad_conv_w: float32 [4, 1792], replicated
- grad_conv_b: float32 [1792], replicated
- grad_dt_bias: float32 [24], replicated
- grad_a_log: float32 [24], replicated
- grad_d_skip: float32 [24], replicated
- grad_gate_gain: float32 [1536], replicated
- grad_w_out: float32 [1536, 768], replicated
Inputs may be any that keep to these rules, and one draw needn't show every extreme that they name: lengths[s] counts the valid slots at the start of sequence s, the rest being padding; at least one sequence is valid in all 4096 slots.
All inputs are finite; a program needn't handle non-finite values.
Results may differ from a plain program's by a relative error of at most 0.012.
The roundings to bfloat16 on the way count: a program that leaves them out, or rounds other values in their place, can miss the bound.
Values may be sent and summed in bfloat16 or wider, within the bound.
A program may use at most 320 MiB of HBM per device.

v0:
```python
from functools import partial
import jax
import jax.numpy as jnp
from jax import lax
from jax.sharding import PartitionSpec as P

INNER = 1536
HEADS = 24
HEAD_DIM = 64
STATE = 128
CONV = 4
BLOCK = 256
SEQS = 2
eps_norm = 1e-05
best = lax.Precision.HIGHEST


def passed_along(value, axis, steps):
    count = lax.axis_size(axis)
    initial, last = (max(0, -steps), min(count, count - steps))
    return lax.ppermute(value, axis, [(source, source + steps) for source in range(initial, last)])


def entering(part, axis, combine, identity, reverse):
    count = lax.axis_size(axis)
    place = lax.axis_index(axis)
    ahead = count - 1 - place if reverse else place
    gathered = jax.tree.map(lambda a: lax.all_gather(a, axis), part)
    state = jax.tree.map(lambda a, e: jnp.zeros_like(a) + jnp.asarray(e, a.dtype), part, identity)

    def one(turn, state):
        source = count - 1 - turn if reverse else turn
        return combine(
            state, jax.tree.map(lambda a: lax.dynamic_index_in_dim(a, source, 0, False), gathered)
        )

    return lax.fori_loop(0, ahead, one, state)


def inverse_rms(values):
    return lax.rsqrt(jnp.mean(values * values, axis=-1, keepdims=True) + eps_norm)


def norm_backward(values, scaling, gain_vec, gradient):
    weighted = gradient * gain_vec
    average = jnp.mean(weighted * values, axis=-1, keepdims=True)
    grad_values = scaling * weighted - values * (scaling * scaling * scaling) * average
    grad_gain = jnp.sum(gradient * values * scaling, axis=0)
    return (grad_values, grad_gain)


def causal_conv(edge_rows, fresh_rows, weights, offset):
    length = fresh_rows.shape[0]
    joined = jnp.concatenate([edge_rows, fresh_rows], axis=0)
    running = offset + joined[0:length] * weights[0]
    for position in range(1, CONV):
        running = running + joined[position : position + length] * weights[position]
    return running


def prepare(
    x_raw,
    bc_raw,
    dt_raw,
    edge_x,
    edge_bc,
    conv_x,
    conv_bc,
    bias_x,
    bias_bc,
    dt_shift,
    a_log_part,
    valid_mask,
):
    keep_mask = valid_mask[:, None]
    x_flat = jax.nn.silu(causal_conv(edge_x, x_raw, conv_x, bias_x)) * keep_mask
    act_bc = jax.nn.silu(causal_conv(edge_bc, bc_raw, conv_bc, bias_bc))
    dt_rows = jax.nn.softplus(dt_raw + dt_shift) * keep_mask
    rates = -jnp.exp(a_log_part)
    x_heads = x_flat.reshape(x_flat.shape[0], -1, HEAD_DIM)
    return (x_heads, act_bc[:, :STATE], act_bc[:, STATE:], dt_rows, rates)


def block_step(rates, carry_state, inputs):
    x_heads, b_rows, c_rows, dt_rows = inputs
    block_len = dt_rows.shape[0]
    cumulative = jnp.cumsum(dt_rows, axis=0) * rates
    indices = jnp.arange(block_len)
    causal = (indices[:, None] >= indices[None, :])[:, :, None]
    spread = cumulative[:, None, :] - cumulative[None, :, :]
    decays = jnp.where(causal, jnp.exp(jnp.where(causal, spread, 0.0)), 0.0)
    scores = jnp.dot(c_rows, b_rows.T, precision=best)
    weight = decays * scores[:, :, None] * dt_rows[None, :, :]
    inner_part = jnp.einsum("tuh,uhp->thp", weight, x_heads, precision=best)
    carried = jnp.exp(cumulative)[:, :, None] * jnp.einsum(
        "tn,hpn->thp", c_rows, carry_state, precision=best
    )
    to_end = jnp.exp(cumulative[-1:] - cumulative) * dt_rows
    fresh_state = jnp.einsum("uh,uhp,un->hpn", to_end, x_heads, b_rows, precision=best)
    carry_state = jnp.exp(cumulative[-1])[:, None, None] * carry_state + fresh_state
    return (carry_state, inner_part + carried)


def mixer(
    valid_mask,
    x_raw,
    bc_raw,
    dt_raw,
    edge_x,
    edge_bc,
    conv_x,
    conv_bc,
    bias_x,
    bias_bc,
    dt_shift,
    a_log_part,
    skip_part,
    incoming,
):
    x_heads, b_rows, c_rows, dt_rows, rates = prepare(
        x_raw,
        bc_raw,
        dt_raw,
        edge_x,
        edge_bc,
        conv_x,
        conv_bc,
        bias_x,
        bias_bc,
        dt_shift,
        a_log_part,
        valid_mask,
    )
    blocks_count = x_heads.shape[0] // BLOCK

    def blocks(values):
        return values.reshape((blocks_count, BLOCK) + values.shape[1:])

    final_state, outputs = lax.scan(
        partial(block_step, rates),
        incoming,
        (blocks(x_heads), blocks(b_rows), blocks(c_rows), blocks(dt_rows)),
    )
    mixed_rows = outputs.reshape(x_heads.shape) + x_heads * skip_part[:, None]
    return (mixed_rows.reshape(x_heads.shape[0], -1), final_state)


def chain(earlier, later):
    return (earlier[0] * later[0], later[0][..., None, None] * earlier[1] + later[1])


def place_into(piece, full_len, start):
    full_shape = piece.shape[:-1] + (full_len,)
    return lax.dynamic_update_slice_in_dim(
        jnp.zeros(full_shape, jnp.float32), piece, start, piece.ndim - 1
    )


def local(
    block_in,
    grad_out,
    lengths,
    norm_gain,
    w_in,
    conv_w,
    conv_b,
    dt_bias,
    a_log,
    d_skip,
    gate_gain,
    w_out,
):
    tokens = block_in.shape[0]
    groups = lax.axis_size("head")
    group_idx = lax.axis_index("head")
    cycle_len = lax.axis_size("seq")
    cycle_idx = lax.axis_index("seq")
    per_seq = cycle_len // SEQS
    heads_here = HEADS // groups
    width_here = heads_here * HEAD_DIM
    local_len = tokens * groups
    cycle_place = cycle_idx // SEQS
    seq_id = cycle_idx % SEQS
    seq_onehot = jnp.arange(SEQS) == seq_id
    seq_valid = jnp.sum(jnp.where(seq_onehot, lengths, 0))
    is_start = cycle_place == 0
    is_last = cycle_place == per_seq - 1
    first_slot = cycle_place * local_len
    valid_heads = (first_slot + jnp.arange(local_len) < seq_valid).astype(jnp.float32)
    valid_tokens = (first_slot + group_idx * tokens + jnp.arange(tokens) < seq_valid).astype(
        jnp.float32
    )
    source = block_in.astype(jnp.float32)
    in_scale = inverse_rms(source)
    normed = (source * in_scale * norm_gain).astype(jnp.bfloat16)
    projected = jnp.dot(normed, w_in, preferred_element_type=jnp.float32).astype(jnp.bfloat16)
    gate_in = projected[:, :INNER].astype(jnp.float32)
    x_part = projected[:, INNER : 2 * INNER].reshape(tokens, groups, width_here)
    bc_part = jnp.broadcast_to(
        projected[:, None, 2 * INNER : 2 * INNER + 2 * STATE], (tokens, groups, 2 * STATE)
    )
    dt_part = projected[:, 2 * INNER + 2 * STATE :].reshape(tokens, groups, heads_here)
    x_raw, bc_raw, dt_raw = (
        lax.all_to_all(x_part, "head", split_axis=1, concat_axis=0, tiled=True),
        lax.all_to_all(bc_part, "head", split_axis=1, concat_axis=0, tiled=True),
        lax.all_to_all(dt_part, "head", split_axis=1, concat_axis=0, tiled=True),
    )
    x_raw = x_raw.reshape(local_len, width_here)
    bc_raw = bc_raw.reshape(local_len, 2 * STATE)
    dt_raw = dt_raw.reshape(local_len, heads_here).astype(jnp.float32)
    tail = local_len - CONV + 1
    edge_x, edge_bc = passed_along((x_raw[tail:], bc_raw[tail:]), "seq", SEQS)
    edge_keep = jnp.where(is_start, 0.0, 1.0)
    edge_x = edge_x.astype(jnp.float32) * edge_keep
    edge_bc = edge_bc.astype(jnp.float32) * edge_keep
    x_raw = x_raw.astype(jnp.float32)
    bc_raw = bc_raw.astype(jnp.float32)
    conv_x = lax.dynamic_slice_in_dim(conv_w, group_idx * width_here, width_here, 1)
    conv_bc = conv_w[:, INNER:]
    bias_x = lax.dynamic_slice_in_dim(conv_b, group_idx * width_here, width_here, 0)
    bias_bc = conv_b[INNER:]
    dt_shift = lax.dynamic_slice_in_dim(dt_bias, group_idx * heads_here, heads_here, 0)
    a_log_part = lax.dynamic_slice_in_dim(a_log, group_idx * heads_here, heads_here, 0)
    skip_part = lax.dynamic_slice_in_dim(d_skip, group_idx * heads_here, heads_here, 0)
    x_heads, b_rows, c_rows, dt_rows, rates = prepare(
        x_raw,
        bc_raw,
        dt_raw,
        edge_x,
        edge_bc,
        conv_x,
        conv_bc,
        bias_x,
        bias_bc,
        dt_shift,
        a_log_part,
        valid_heads,
    )
    cumulative = jnp.cumsum(dt_rows, axis=0) * rates
    decay_all = jnp.exp(cumulative[-1])
    to_end = jnp.exp(cumulative[-1:] - cumulative) * dt_rows
    own_state = jnp.einsum("uh,uhp,un->hpn", to_end, x_heads, b_rows, precision=best)
    slot_mask = seq_onehot.astype(jnp.float32)
    identity = (
        jnp.ones((SEQS, heads_here), jnp.float32),
        jnp.zeros((SEQS, heads_here, HEAD_DIM, STATE), jnp.float32),
    )

    def slotted(decay_vec, piece_state):
        decay_slots = jnp.where(seq_onehot[:, None], decay_vec[None, :], 1.0)
        state_slots = slot_mask[:, None, None, None] * piece_state[None]
        return (decay_slots, state_slots)

    arrived_all = entering(
        slotted(jnp.where(is_start, 0.0, decay_all), own_state), "seq", chain, identity, False
    )[1]
    arrived = lax.dynamic_index_in_dim(arrived_all, seq_id, 0, keepdims=False)
    incoming = jnp.where(is_start, 0.0, arrived)
    (mixed_heads, final_state), pull_back = jax.vjp(
        partial(mixer, valid_heads),
        x_raw,
        bc_raw,
        dt_raw,
        edge_x,
        edge_bc,
        conv_x,
        conv_bc,
        bias_x,
        bias_bc,
        dt_shift,
        a_log_part,
        skip_part,
        incoming,
    )
    mixed_send = mixed_heads.astype(jnp.bfloat16).reshape(local_len, 1, width_here)
    mixed_tok = (
        lax.all_to_all(mixed_send, "head", split_axis=0, concat_axis=1, tiled=True)
        .reshape(tokens, INNER)
        .astype(jnp.float32)
    )
    gate_sigmoid = jax.nn.sigmoid(gate_in)
    gate_act = gate_in * gate_sigmoid
    gated = mixed_tok * gate_act
    gate_scale = inverse_rms(gated)
    gnormed = (gated * gate_scale * gate_gain).astype(jnp.bfloat16)
    branch = jnp.dot(gnormed, w_out, preferred_element_type=jnp.float32)
    valid_col = valid_tokens[:, None]
    block_out = (source + valid_col * branch).astype(jnp.bfloat16)
    grad_rows = grad_out.astype(jnp.float32)
    d_branch = (grad_rows * valid_col).astype(jnp.bfloat16)
    grad_w_out = jnp.einsum("ti,td->id", gnormed, d_branch, preferred_element_type=jnp.float32)
    d_gnormed = jnp.einsum("td,id->ti", d_branch, w_out, preferred_element_type=jnp.float32)
    d_gated, grad_gate = norm_backward(gated, gate_scale, gate_gain, d_gnormed)
    d_mixed = (d_gated * gate_act).astype(jnp.bfloat16)
    d_gate_in = d_gated * mixed_tok * gate_sigmoid * (1.0 + gate_in * (1.0 - gate_sigmoid))
    d_heads = lax.all_to_all(
        d_mixed.reshape(tokens, groups, width_here), "head", split_axis=1, concat_axis=0, tiled=True
    )
    d_heads = d_heads.reshape(local_len, width_here).astype(jnp.float32)
    weighted = d_heads.reshape(local_len, heads_here, HEAD_DIM) * jnp.exp(cumulative)[:, :, None]
    own_grad = jnp.einsum("thp,tn->hpn", weighted, c_rows, precision=best)
    behind_all = entering(
        slotted(jnp.where(is_last, 0.0, decay_all), own_grad), "seq", chain, identity, True
    )[1]
    behind = lax.dynamic_index_in_dim(behind_all, seq_id, 0, keepdims=False)
    from_right = jnp.where(is_last, 0.0, behind)
    grads = pull_back((d_heads, from_right))
    back_x, back_bc = passed_along((grads[3] * edge_keep, grads[4] * edge_keep), "seq", -SEQS)
    dx_heads = jnp.concatenate([grads[0][:tail], grads[0][tail:] + back_x], axis=0)
    dbc_heads = jnp.concatenate([grads[1][:tail], grads[1][tail:] + back_bc], axis=0)
    rec_x, rec_bc, rec_dt = (
        lax.all_to_all(
            dx_heads.reshape(local_len, 1, width_here),
            "head",
            split_axis=0,
            concat_axis=1,
            tiled=True,
        ),
        lax.all_to_all(
            dbc_heads.reshape(local_len, 1, 2 * STATE),
            "head",
            split_axis=0,
            concat_axis=1,
            tiled=True,
        ),
        lax.all_to_all(
            grads[2].reshape(local_len, 1, heads_here),
            "head",
            split_axis=0,
            concat_axis=1,
            tiled=True,
        ),
    )
    d_projected = jnp.concatenate(
        [
            d_gate_in,
            rec_x.reshape(tokens, INNER),
            jnp.sum(rec_bc, axis=1),
            rec_dt.reshape(tokens, HEADS),
        ],
        axis=1,
    ).astype(jnp.bfloat16)
    grad_w_in = jnp.einsum("td,tp->dp", normed, d_projected, preferred_element_type=jnp.float32)
    d_normed = jnp.einsum("tp,dp->td", d_projected, w_in, preferred_element_type=jnp.float32)
    d_source, grad_norm = norm_backward(source, in_scale, norm_gain, d_normed)
    grad_in = grad_rows + d_source
    grad_conv = jnp.concatenate(
        [place_into(grads[5], INNER, group_idx * width_here), grads[6]], axis=1
    )
    grad_bias = jnp.concatenate(
        [place_into(grads[7], INNER, group_idx * width_here), grads[8]], axis=0
    )
    grad_dt = place_into(grads[9], HEADS, group_idx * heads_here)
    grad_alog = place_into(grads[10], HEADS, group_idx * heads_here)
    grad_skip = place_into(grads[11], HEADS, group_idx * heads_here)
    (
        grad_norm,
        grad_w_in,
        grad_conv,
        grad_bias,
        grad_dt,
        grad_alog,
        grad_skip,
        grad_gate,
        grad_w_out,
    ) = lax.psum(
        (
            grad_norm,
            grad_w_in,
            grad_conv,
            grad_bias,
            grad_dt,
            grad_alog,
            grad_skip,
            grad_gate,
            grad_w_out,
        ),
        ("seq", "head"),
    )
    return (
        block_out,
        grad_in,
        grad_norm,
        grad_w_in,
        grad_conv,
        grad_bias,
        grad_dt,
        grad_alog,
        grad_skip,
        grad_gate,
        grad_w_out,
    )


def solution(mesh):
    placed = (
        P(("seq", "head"), None),
        P(("seq", "head"), None),
        P(),
        P(),
        P(),
        P(),
        P(),
        P(),
        P(),
        P(),
        P(),
        P(),
    )
    return jax.shard_map(
        local,
        mesh=mesh,
        in_specs=placed,
        out_specs=(
            P(("seq", "head"), None),
            P(("seq", "head"), None),
            P(),
            P(),
            P(),
            P(),
            P(),
            P(),
            P(),
            P(),
            P(),
        ),
        check_vma=False,
    )
```

profile of v0, /device:TPU:0, one launch (start us, length us, event | category | flops | bytes accessed | tf_op | source)
XLA Modules:
  0.0 1019.1 jit_solution(1937852641391881275)
XLA Ops:
  9.1 4.2 convolution_convert_fusion
  15.8 5.6 all_to_all.103
  22.0 5.5 collective-permute-start
  28.3 3.4 all-to-all-start.2
  33.3 3.2 all-to-all-start
  37.2 3.4 collective-permute-start.1
  61.8 3.1 copy.239
  70.4 37.2 %all_gather.16 = f32[16,2,12]{2,1,0:T(2,128)S(1)} all-gather(f32[1,2,12]{2,1,0:T(2,128)S(1)} %get-tuple-element.2016), channel_id=1, replica_groups=mesh['seq'=16,'head'=2] {'seq'}, dimensions={0}, use_global_device_ids=true | all-gather | bytes 1632 | tf_op jit(solution)/shard_map/all_gather | solution.py:28
  112.4 3.1 reshape.715
  118.3 102.5 %all-gather.3.cloned.1.call-done = f32[16,2,12,64,128]{4,3,2,1,0:T(8,128)} async-done(((f32[1,2,12,64,128]{4,3,2,1,0:T(8,128)}), f32[16,2,12,64,128]{4,3,2,1,0:T(8,128)}) %all-gather.3.cloned.1.call-update) | async-done | bytes 12582928 | tf_op jit(solution)/shard_map/all_gather | solution.py:28
  224.6 80.5 %while.105 = (s32[]{:T(128)}, f32[12,64,128]{2,1,0:T(8,128)S(1)}, f32[2,256,12,64]{1,0,3,2:T(2,128)}, f32[2,256,12]{1,2,0:T(8,128)S(1)}, f32[2,256,256,12]{2,1,3...) while((s32[]{:T(128)}, f32[12,64,128]{2,1,0:T(8,128)S(1)}, ...), condition=%wide.region_9.10_spmd.clone.clone, body=%wide.region_6.9_spmd.clone.clone.sunk | while | flops 1317872640 | bytes 61413468 | solution.py:139
  235.0 3.8 fusion.240
  239.6 16.7 %dynamic_update_slice.270 = f32[2,256,12,64]{1,0,3,2:T(2,128)} dynamic-update-slice(f32[2,256,12,64]{1,0,3,2:T(2,128)} %get-tuple-element.2536, f32[1,256,12,64]{1,0,3,2:T(1,128)S(1)} %copy.345, s32[]{:T(128)S(6)} %copy.400, s32[]{:T(128)} %constant.277.clone.1..sunk.2, s32[]{:T(128)} %constant.277.clone.1..sunk.2, s32[]{:T(128)} %constant.277.clone.1..sunk.2) | dynamic-update-slice | bytes 1572868 | tf_op jit(solution)/shard_map/jvp()/while/body/jit(dynamic_update_index_in_dim)/dynamic_update_slice | solution.py:139
  256.3 6.3 multiply_dynamic-update-slice_fusion.3
  275.3 3.8 fusion.240
  279.8 16.7 %dynamic_update_slice.270 = f32[2,256,12,64]{1,0,3,2:T(2,128)} dynamic-update-slice(f32[2,256,12,64]{1,0,3,2:T(2,128)} %get-tuple-element.2536, f32[1,256,12,64]{1,0,3,2:T(1,128)S(1)} %copy.345, s32[]{:T(128)S(6)} %copy.400, s32[]{:T(128)} %constant.277.clone.1..sunk.2, s32[]{:T(128)} %constant.277.clone.1..sunk.2, s32[]{:T(128)} %constant.277.clone.1..sunk.2) | dynamic-update-slice | bytes 1572868 | tf_op jit(solution)/shard_map/jvp()/while/body/jit(dynamic_update_index_in_dim)/dynamic_update_slice | solution.py:139
  296.6 6.3 multiply_dynamic-update-slice_fusion.3
  307.9 3.0 copy.244
  317.8 5.8 all_to_all.104
  328.0 3.0 copy.247
  340.3 5.4 all_to_all.105
  347.8 3.7 copy.250
  351.5 3.4 reshape.748
  359.6 58.6 %all_gather.18 = f32[16,2,12]{2,1,0:T(2,128)S(1)} all-gather(f32[1,2,12]{2,1,0:T(2,128)S(1)} %copy-done.141), channel_id=1, replica_groups=mesh['seq'=16,'head'=2] {'seq'}, dimensions={0}, use_global_device_ids=true | all-gather | bytes 1632 | tf_op jit(solution)/shard_map/all_gather | solution.py:28
  418.2 3.0 copy.251
  421.2 4.5 fusion.160
  425.7 103.9 %all-gather.5.cloned.1.call-done = f32[16,2,12,64,128]{4,3,2,1,0:T(8,128)} async-done(((f32[1,2,12,64,128]{4,3,2,1,0:T(8,128)}), f32[16,2,12,64,128]{4,3,2,1,0:T(8,128)}) %all-gather.5.cloned.1.call-update) | async-done | bytes 12582928 | tf_op jit(solution)/shard_map/all_gather | solution.py:28
  529.6 20.4 %while.104 = (s32[]{:T(128)}, f32[2,12,64,128]{3,2,1,0:T(8,128)S(1)}, s32[]{:T(128)}, f32[16,2,12]{2,1,0:T(2,128)S(1)}, f32[16,2,12,64,128]{4,3,2,1,0:T(8,128)},...) while((s32[]{:T(128)}, f32[2,12,64,128]{3,2,1,0:T(8,128)S(1)}, s32[]{:T(128)}, ...), condition=%wide.region_13.14_spmd, body=%wide.region_12.13_spmd.sunk | while | flops 393222 | bytes 2359739 | solution.py:37
  554.0 121.2 %while.106 = (s32[]{:T(128)}, f32[12]{0:T(128)}, f32[12,64,128]{2,1,0:T(8,128)S(1)}, f32[2,256,12,64]{1,0,3,2:T(2,128)}, f32[2,256,128]{2,1,0:T(8,128)}, /*index...) while((s32[]{:T(128)}, f32[12]{0:T(128)}, ...), condition=%wide.region_25.26_spmd.clone.clone, body=%wide.region_14.25_spmd.clone.clone.sunk | while | flops 2628298752 | bytes 62654428 | solution.py:139
  555.8 9.5 fusion.254
  577.4 3.2 convolution_bitcast_fusion.4
  584.2 4.0 fusion.262
  589.0 16.7 %dynamic_update_slice.275 = f32[2,256,12,64]{1,0,3,2:T(2,128)} dynamic-update-slice(f32[2,256,12,64]{1,0,3,2:T(2,128)} %get-tuple-element.2656, f32[1,256,12,64]{1,0,3,2:T(1,128)S(1)} %copy.348, s32[]{:T(128)S(6)} %sub.279, s32[]{:T(128)} %constant.277.clone.1..sunk.3, s32[]{:T(128)} %constant.277.clone.1..sunk.3, s32[]{:T(128)} %constant.277.clone.1..sunk.3) | dynamic-update-slice | bytes 1572868 | tf_op jit(solution)/shard_map/transpose(jvp())/while/body/jit(dynamic_update_index_in_dim)/dynamic_update_slice | solution.py:139
  616.3 9.5 fusion.254
  637.9 3.2 convolution_bitcast_fusion.4
  644.5 4.0 fusion.262
  649.3 16.7 %dynamic_update_slice.275 = f32[2,256,12,64]{1,0,3,2:T(2,128)} dynamic-update-slice(f32[2,256,12,64]{1,0,3,2:T(2,128)} %get-tuple-element.2656, f32[1,256,12,64]{1,0,3,2:T(1,128)S(1)} %copy.348, s32[]{:T(128)S(6)} %sub.279, s32[]{:T(128)} %constant.277.clone.1..sunk.3, s32[]{:T(128)} %constant.277.clone.1..sunk.3, s32[]{:T(128)} %constant.277.clone.1..sunk.3) | dynamic-update-slice | bytes 1572868 | tf_op jit(solution)/shard_map/transpose(jvp())/while/body/jit(dynamic_update_index_in_dim)/dynamic_update_slice | solution.py:139
  684.0 3.1 copy.255
  687.1 6.1 multiply_reduce_fusion.3
  698.6 3.7 all_to_all.106
  711.1 4.2 all_to_all.107
  720.4 5.2 all_to_all.108
  733.0 6.8 fusion.156
  740.7 3.2 fusion.138
  745.8 5.9 fusion.148
  751.7 45.2 %all-reduce.20 = (f32[768]{0:T(1024)}, f32[4,1792]{1,0:T(4,128)}, f32[1792]{0:T(1024)}, f32[24]{0:T(128)}, f32[24]{0:T(128)}, /*index=5*/f32[24]{0:T(128)}, f32[1536]{0:T(1024)}) all-reduce(f32[768]{0:T(1024)S(1)} %get-tuple-element.1806, f32[4,1792]{1,0:T(4,128)S(1)} %pad_maximum_fusion.5, ...), channel_id=1, replica_groups=mesh['seq'=16,'head'=2] {'seq','head'}, use_global_device_ids=true, to_apply=%region_29.30 | all-reduce | flops 11336 | bytes 90688 | tf_op jit(solution)/shard_map/psum | solution.py:366
  799.2 201.9 %all-reduce.24.cloned.1.call-done = (f32[768,3352]{0,1:T(8,128)}, f32[1536,768]{1,0:T(8,128)}) async-done(((f32[768,3352]{0,1:T(8,128)}, f32[1536,768]{1,0:T(8,128)}), (f32[768,3352]{0,1:T(8,128)}, f32[1536,768]{1,0:T(8,128)})) %all-reduce.24.cloned.1.call-update) | async-done | bytes 15015952 | tf_op jit(solution)/shard_map/psum | solution.py:366
  1001.1 8.8 copy.483
  (722 shorter events, 221.4 us)
Async XLA Ops:
  7.2 326.1 %copy-start = (bf16[1536,768]{1,0:T(8,128)(2,1)S(1)}, bf16[1536,768]{1,0:T(8,128)(2,1)}, u32[]{:S(2)}) copy-start(bf16[1536,768]{1,0:T(8,128)(2,1)} %param.31) | copy-start | bytes 7077892
  14.6 12.8 %slice-start = ((bf16[256,3352]{0,1:T(8,128)(2,1)}), bf16[256,256]{0,1:T(8,128)(2,1)S(1)}, s32[]{:S(2)}) async-start(bf16[256,3352]{0,1:T(8,128)(2,1)} %copy-done.40), calls=%async_computation.11 | async-start | bytes 262144 | tf_op jit(solution)/shard_map/slice | solution.py:200
  15.8 16.0 %slice-start.1 = ((bf16[256,3352]{0,1:T(8,128)(2,1)}), bf16[256,24]{0,1:T(8,128)(2,1)S(1)}, s32[]{:S(2)}) async-start(bf16[256,3352]{0,1:T(8,128)(2,1)} %copy-done.40), calls=%async_computation.12 | async-start | bytes 24576 | tf_op jit(solution)/shard_map/slice | solution.py:202
  15.8 25.3 %copy-start.149 = (s32[2]{0:T(128)S(1)}, s32[2]{0:T(128)}, u32[]{:S(2)}) copy-start(s32[2]{0:T(128)} %param.22) | copy-start | bytes 28
  21.4 31.6 %copy-start.28 = (bf16[256,2,768]{2,0,1:T(8,128)(2,1)}, bf16[256,2,768]{2,0,1:T(8,128)(2,1)S(1)}, u32[]{:S(2)}) copy-start(bf16[256,2,768]{2,0,1:T(8,128)(2,1)S(1)} %all_to_all.103) | copy-start | bytes 2359300
  22.0 36.4 %collective-permute-start = (bf16[3,768]{1,0:T(4,128)(2,1)}, bf16[3,768]{1,0:T(4,128)(2,1)}, u32[]{:S(2)}, u32[]{:S(2)}) collective-permute-start(bf16[3,768]{1,0:T(4,128)(2,1)} %slice.198), channel_id=1, source_target_pairs={{0,4},{2,6},{4,8},{6,10},{8,12},{10,14},{12,16},{14,18},{16,20},{1... | collective-permute-start | bytes 13832 | tf_op jit(solution)/shard_map/ppermute | solution.py:21
  28.3 5.0 all-to-all-start.2
  33.3 19.7 %copy-start.46 = (bf16[256,2,256]{2,0,1:T(8,128)(2,1)}, bf16[256,2,256]{2,0,1:T(8,128)(2,1)S(1)}, u32[]{:S(2)}) copy-start(bf16[256,2,256]{2,0,1:T(8,128)(2,1)S(1)} %all-to-all-done.2) | copy-start | bytes 786436
  33.3 8.5 all-to-all-start
  36.5 184.3 %all-gather.3.cloned.1.call-start = ((), (), s32[]{:S(2)}) async-start(), calls=%async_computation.8 | async-start | bytes 13369344 | tf_op jit(solution)/shard_map/all_gather | solution.py:28
  37.2 17.7 %collective-permute-start.1 = (bf16[3,256]{1,0:T(4,128)(2,1)}, bf16[3,256]{1,0:T(4,128)(2,1)}, u32[]{:S(2)}, u32[]{:S(2)}) collective-permute-start(bf16[3,256]{1,0:T(4,128)(2,1)} %slice.204), channel_id=1, source_target_pairs={{0,4},{2,6},{4,8},{6,10},{8,12},{10,14},{12,16},{14,18},{16,20},{1... | collective-permute-start | bytes 4616 | tf_op jit(solution)/shard_map/ppermute | solution.py:21
  41.7 69.1 %copy-start.77 = (bf16[256,2,12]{0,2,1:T(8,128)(2,1)}, bf16[256,2,12]{0,2,1:T(8,128)(2,1)S(1)}, u32[]{:S(2)}) copy-start(bf16[256,2,12]{0,2,1:T(8,128)(2,1)S(1)} %all-to-all-done) | copy-start | bytes 36868
  41.7 11.2 %copy-start.71 = (f32[2,256,1,12]{1,3,0,2:T(8,128)}, f32[2,256,1,12]{1,3,0,2:T(8,128)S(1)}, u32[]{:S(2)}) copy-start(f32[2,256,1,12]{1,3,0,2:T(8,128)S(1)} %convert_bitcast_fusion.3) | copy-start | bytes 73732
  42.5 16.7 %copy-start.91 = (f32[512]{0:T(512)}, f32[512]{0:T(512)S(1)}, u32[]{:S(2)}) copy-start(f32[512]{0:T(512)S(1)} %fusion.181) | copy-start | bytes 6148
  43.2 9.7 copy-start.121
  54.9 6.9 copy-start.103
  54.9 6.9 copy-start.105
  54.9 6.9 copy-start.107
  54.9 6.9 copy-start.109
  58.4 53.2 %copy-start.35 = (f32[512,256]{1,0:T(8,128)}, f32[512,256]{1,0:T(8,128)S(1)}, u32[]{:S(2)}) copy-start(f32[512,256]{1,0:T(8,128)S(1)} %get-tuple-element.1976) | copy-start | bytes 1572868
  67.8 39.9 %copy-start.147 = (f32[24]{0:T(128)S(1)}, f32[24]{0:T(128)}, u32[]{:S(2)}) copy-start(f32[24]{0:T(128)} %param.28) | copy-start | bytes 292
  67.8 43.1 %copy-start.122 = (f32[12]{0:T(128)S(1)}, f32[12]{0:T(128)}, u32[]{:S(2)}) copy-start(f32[12]{0:T(128)} %copy-done.121) | copy-start | bytes 148
  68.9 460.7 %all-gather.5.cloned.1.call-start = ((), (), s32[]{:S(2)}) async-start(), calls=%async_computation.9 | async-start | bytes 13369344 | tf_op jit(solution)/shard_map/all_gather | solution.py:28
  228.1 6.9 copy-start.18
  333.3 87.9 %copy-start.98 = (f32[256]{0:T(256)}, f32[256]{0:T(256)S(1)}, u32[]{:S(2)}) copy-start(f32[256]{0:T(256)S(1)} %get-tuple-element.2014) | copy-start | bytes 3076
  358.9 642.3 %all-reduce.24.cloned.1.call-start = ((), (), s32[]{:S(2)}) async-start(), calls=%async_computation.10 | async-start | bytes 30031872 | tf_op jit(solution)/shard_map/psum | solution.py:366
  555.8 9.5 copy-start.1
  555.8 9.5 copy-start.21
  555.8 10.2 %copy-start.11 = (f32[2,256,128]{2,1,0:T(8,128)S(1)}, f32[2,256,128]{2,1,0:T(8,128)}, u32[]{:S(2)}) copy-start(f32[2,256,128]{2,1,0:T(8,128)} %get-tuple-element.2697) | copy-start | bytes 786436 | tf_op jit(solution)/shard_map/transpose(jvp())/while
  576.1 8.0 copy-start.70
  576.1 8.0 copy-start.2
  605.7 8.3 copy-start.51
  605.7 8.3 copy-start.63
  605.7 8.3 copy-start.73
  616.3 9.5 copy-start.1
  616.3 9.5 copy-start.21
  616.3 10.2 %copy-start.11 = (f32[2,256,128]{2,1,0:T(8,128)S(1)}, f32[2,256,128]{2,1,0:T(8,128)}, u32[]{:S(2)}) copy-start(f32[2,256,128]{2,1,0:T(8,128)} %get-tuple-element.2697) | copy-start | bytes 786436 | tf_op jit(solution)/shard_map/transpose(jvp())/while
  636.6 7.9 copy-start.70
  636.6 7.9 copy-start.2
  666.1 8.3 copy-start.51
  666.1 8.3 copy-start.63
  666.1 8.3 copy-start.73
  680.0 29.8 %collective-permute-start.3 = (f32[3,256]{1,0:T(4,128)}, f32[3,256]{1,0:T(4,128)}, u32[]{:S(2)}, u32[]{:S(2)}) collective-permute-start(f32[3,256]{1,0:T(4,128)} %add_multiply_fusion.1), channel_id=1, source_target_pairs={{4,0},{6,2},{8,4},{10,6},{12,8},{14,10},{16,12},{18,14},{20,16},{2... | collective-permute-start | bytes 9224 | tf_op jit(solution)/shard_map/ppermute | solution.py:21
  698.6 7.7 copy-start.126
  706.3 9.8 collective-permute-start.2
  745.8 51.1 %copy-start.43 = (bf16[256,768]{1,0:T(8,128)(2,1)S(1)}, bf16[256,768]{1,0:T(8,128)(2,1)}, u32[]{:S(2)}) copy-start(bf16[256,768]{1,0:T(8,128)(2,1)} %param.21) | copy-start | bytes 1179652
  745.8 51.1 %copy-start.135 = (f32[256]{0:T(256)S(1)}, f32[256]{0:T(256)}, u32[]{:S(2)}) copy-start(f32[256]{0:T(256)} %get-tuple-element.2011) | copy-start | bytes 3076
  1001.1 8.8 copy-start.34
  (163 other events, 547.8 us)
Sparse Core Ops, SparseCore 0:
  69.0 151.7 all-gather.2
  359.0 170.5 all-gather.4
  740.0 261.1 all-reduce.23
where the time goes:
time: 1030 us; the launch traced here: 1020 us
  waiting for transfers between devices  409 us (40%)
  local copies, waits for them, and re-layouts  185 us (18%)
  blocking collectives  171 us (17%)
  other arithmetic  118 us (11%)
  matrix products  99.5 us (10%)
  starting transfers between devices  18.3 us (2%)
  between operations  15.6 us (2%)
    all_gather x2, waiting for transfers between devices, entering(): gathered = jax.tree.map(lambda a: lax.all_gather(a, axis), part)  206 us
    psum x1, waiting for transfers between devices, local(): lax.psum((grad_norm, grad_w_in, grad_conv, grad_bias, grad_dt, grad_alog,...  202 us
    all_gather x2, blocking collectives, entering(): gathered = jax.tree.map(lambda a: lax.all_gather(a, axis), part)  95.8 us
    dynamic_update_slice x18, local copies, waits for them, and re-layouts, mixer(): lax.scan(partial(block_step, rates), incoming, (blocks(x_heads), blocks(b...  71.9 us
    psum x1, blocking collectives, local(): lax.psum((grad_norm, grad_w_in, grad_conv, grad_bias, grad_dt, grad_alog,...  45.2 us
    dot_general x6, matrix products, block_step(): inner_part = jnp.einsum('tuh,uhp->thp', weight, x_heads, precision=best)  34.4 us
    unnamed x229, local copies, waits for them, and re-layouts  32.9 us
  transfers between devices with their start and end apart: 9, of which 4 were waited for; matrix products, arithmetic and copies ran while one was open for 8% of the time, Pallas kernels for 0%

commit v1 on v0

--- a/solution.py
+++ b/solution.py
@@ -364,18 +364,21 @@
         grad_gate,
         grad_w_out,
     ) = lax.psum(
-        (
-            grad_norm,
-            grad_w_in,
-            grad_conv,
-            grad_bias,
-            grad_dt,
-            grad_alog,
-            grad_skip,
-            grad_gate,
-            grad_w_out,
+        lax.psum(
+            (
+                grad_norm,
+                grad_w_in,
+                grad_conv,
+                grad_bias,
+                grad_dt,
+                grad_alog,
+                grad_skip,
+                grad_gate,
+                grad_w_out,
+            ),
+            "head",
         ),
-        ("seq", "head"),
+        "seq",
     )
     return (
         block_out,

time: 1030 us -> 1250 us (1.21)
  waiting for transfers between devices: 409 us -> 588 us
  blocking collectives: 171 us -> 212 us
    psum x0 -> x1, waiting for transfers between devices: none -> 326 us  [local(): lax.psum(lax.psum((grad_norm, grad_w_in, grad_conv, grad_bias, grad_dt, g...]
    psum x1, waiting for transfers between devices: 202 us -> 54.5 us  [local(): lax.psum((grad_norm, grad_w_in, grad_conv, grad_bias, grad_dt, grad_alog,...]
    psum x0 -> x1, blocking collectives: none -> 82.6 us  [local(): lax.psum(lax.psum((grad_norm, grad_w_in, grad_conv, grad_bias, grad_dt, g...]
    psum x1, blocking collectives: 45.2 us -> 3.69 us  [local(): lax.psum((grad_norm, grad_w_in, grad_conv, grad_bias, grad_dt, grad_alog,...]
  transfers between devices with their start and end apart: 9 -> 10, of which waited for: 4 -> 5; matrix products, arithmetic and copies ran while one was open for 8% -> 6% of each run, Pallas kernels for 0% -> 0%
where the time goes in v1:
time: 1250 us; the launch traced here: 1240 us
  waiting for transfers between devices  588 us (47%)
  blocking collectives  212 us (17%)
  local copies, waits for them, and re-layouts  185 us (15%)
  other arithmetic  118 us (9%)
  matrix products  99.2 us (8%)
  starting transfers between devices  18.3 us (1%)
  between operations  15.6 us (1%)
    psum x1, waiting for transfers between devices, local(): lax.psum(lax.psum((grad_norm, grad_w_in, grad_conv, grad_bias, grad_dt, g...  326 us
    all_gather x2, waiting for transfers between devices, entering(): gathered = jax.tree.map(lambda a: lax.all_gather(a, axis), part)  206 us
    all_gather x2, blocking collectives, entering(): gathered = jax.tree.map(lambda a: lax.all_gather(a, axis), part)  95.8 us
    psum x1, blocking collectives, local(): lax.psum(lax.psum((grad_norm, grad_w_in, grad_conv, grad_bias, grad_dt, g...  82.6 us
    dynamic_update_slice x18, local copies, waits for them, and re-layouts, mixer(): lax.scan(partial(block_step, rates), incoming, (blocks(x_heads), blocks(b...  71.9 us
    psum x1, waiting for transfers between devices, local(): lax.psum((grad_norm, grad_w_in, grad_conv, grad_bias, grad_dt, grad_alog,...  54.5 us
    dot_general x6, matrix products, block_step(): inner_part = jnp.einsum('tuh,uhp->thp', weight, x_heads, precision=best)  34.4 us
    unnamed x229, local copies, waits for them, and re-layouts  32.9 us
  transfers between devices with their start and end apart: 10, of which 5 were waited for; matrix products, arithmetic and copies ran while one was open for 6% of the time, Pallas kernels for 0%

profile of v1, /device:TPU:0, one launch (start us, length us, event | category | flops | bytes accessed | tf_op | source)
XLA Modules:
  0.0 1238.9 jit_solution(9972777307855817055)
XLA Ops:
  9.1 4.2 convolution_convert_fusion
  15.8 5.6 all_to_all.103
  22.0 5.5 collective-permute-start
  28.3 3.4 all-to-all-start.2
  33.3 3.2 all-to-all-start
  37.2 3.4 collective-permute-start.1
  61.8 3.1 copy.239
  70.4 37.2 %all_gather.16 = f32[16,2,12]{2,1,0:T(2,128)S(1)} all-gather(f32[1,2,12]{2,1,0:T(2,128)S(1)} %get-tuple-element.2025), channel_id=1, replica_groups=mesh['seq'=16,'head'=2] {'seq'}, dimensions={0}, use_global_device_ids=true | all-gather | bytes 1632 | tf_op jit(solution)/shard_map/all_gather | solution.py:28
  112.4 3.1 reshape.715
  118.3 102.5 %all-gather.3.cloned.1.call-done = f32[16,2,12,64,128]{4,3,2,1,0:T(8,128)} async-done(((f32[1,2,12,64,128]{4,3,2,1,0:T(8,128)}), f32[16,2,12,64,128]{4,3,2,1,0:T(8,128)}) %all-gather.3.cloned.1.call-update) | async-done | bytes 12582928 | tf_op jit(solution)/shard_map/all_gather | solution.py:28
  224.6 80.5 %while.105 = (s32[]{:T(128)}, f32[12,64,128]{2,1,0:T(8,128)S(1)}, f32[2,256,12,64]{1,0,3,2:T(2,128)}, f32[2,256,12]{1,2,0:T(8,128)S(1)}, f32[2,256,256,12]{2,1,3...) while((s32[]{:T(128)}, f32[12,64,128]{2,1,0:T(8,128)S(1)}, ...), condition=%wide.region_9.10_spmd.clone.clone, body=%wide.region_6.9_spmd.clone.clone.sunk | while | flops 1317872640 | bytes 61413468 | solution.py:139
  235.0 3.8 fusion.240
  239.6 16.7 %dynamic_update_slice.270 = f32[2,256,12,64]{1,0,3,2:T(2,128)} dynamic-update-slice(f32[2,256,12,64]{1,0,3,2:T(2,128)} %get-tuple-element.2545, f32[1,256,12,64]{1,0,3,2:T(1,128)S(1)} %copy.345, s32[]{:T(128)S(6)} %copy.400, s32[]{:T(128)} %constant.277.clone.1..sunk.2, s32[]{:T(128)} %constant.277.clone.1..sunk.2, s32[]{:T(128)} %constant.277.clone.1..sunk.2) | dynamic-update-slice | bytes 1572868 | tf_op jit(solution)/shard_map/jvp()/while/body/jit(dynamic_update_index_in_dim)/dynamic_update_slice | solution.py:139
  256.3 6.3 multiply_dynamic-update-slice_fusion.3
  275.3 3.8 fusion.240
  279.8 16.7 %dynamic_update_slice.270 = f32[2,256,12,64]{1,0,3,2:T(2,128)} dynamic-update-slice(f32[2,256,12,64]{1,0,3,2:T(2,128)} %get-tuple-element.2545, f32[1,256,12,64]{1,0,3,2:T(1,128)S(1)} %copy.345, s32[]{:T(128)S(6)} %copy.400, s32[]{:T(128)} %constant.277.clone.1..sunk.2, s32[]{:T(128)} %constant.277.clone.1..sunk.2, s32[]{:T(128)} %constant.277.clone.1..sunk.2) | dynamic-update-slice | bytes 1572868 | tf_op jit(solution)/shard_map/jvp()/while/body/jit(dynamic_update_index_in_dim)/dynamic_update_slice | solution.py:139
  296.6 6.3 multiply_dynamic-update-slice_fusion.3
  307.9 3.0 copy.244
  317.8 5.8 all_to_all.104
  340.3 5.4 all_to_all.105
  347.8 3.7 copy.250
  351.5 3.4 reshape.748
  359.6 58.6 %all_gather.18 = f32[16,2,12]{2,1,0:T(2,128)S(1)} all-gather(f32[1,2,12]{2,1,0:T(2,128)S(1)} %copy-done.141), channel_id=1, replica_groups=mesh['seq'=16,'head'=2] {'seq'}, dimensions={0}, use_global_device_ids=true | all-gather | bytes 1632 | tf_op jit(solution)/shard_map/all_gather | solution.py:28
  421.2 4.5 fusion.160
  425.7 103.9 %all-gather.5.cloned.1.call-done = f32[16,2,12,64,128]{4,3,2,1,0:T(8,128)} async-done(((f32[1,2,12,64,128]{4,3,2,1,0:T(8,128)}), f32[16,2,12,64,128]{4,3,2,1,0:T(8,128)}) %all-gather.5.cloned.1.call-update) | async-done | bytes 12582928 | tf_op jit(solution)/shard_map/all_gather | solution.py:28
  529.6 20.4 %while.104 = (s32[]{:T(128)}, f32[2,12,64,128]{3,2,1,0:T(8,128)S(1)}, s32[]{:T(128)}, f32[16,2,12]{2,1,0:T(2,128)S(1)}, f32[16,2,12,64,128]{4,3,2,1,0:T(8,128)},...) while((s32[]{:T(128)}, f32[2,12,64,128]{3,2,1,0:T(8,128)S(1)}, s32[]{:T(128)}, ...), condition=%wide.region_13.14_spmd, body=%wide.region_12.13_spmd.sunk | while | flops 393222 | bytes 2359739 | solution.py:37
  554.0 121.2 %while.106 = (s32[]{:T(128)}, f32[12]{0:T(128)}, f32[12,64,128]{2,1,0:T(8,128)S(1)}, f32[2,256,12,64]{1,0,3,2:T(2,128)}, f32[2,256,128]{2,1,0:T(8,128)}, /*index...) while((s32[]{:T(128)}, f32[12]{0:T(128)}, ...), condition=%wide.region_25.26_spmd.clone.clone, body=%wide.region_14.25_spmd.clone.clone.sunk | while | flops 2628298752 | bytes 62654428 | solution.py:139
  555.8 9.5 fusion.254
  577.4 3.2 convolution_bitcast_fusion.4
  584.2 4.0 fusion.262
  589.0 16.7 %dynamic_update_slice.275 = f32[2,256,12,64]{1,0,3,2:T(2,128)} dynamic-update-slice(f32[2,256,12,64]{1,0,3,2:T(2,128)} %get-tuple-element.2665, f32[1,256,12,64]{1,0,3,2:T(1,128)S(1)} %copy.348, s32[]{:T(128)S(6)} %sub.279, s32[]{:T(128)} %constant.277.clone.1..sunk.3, s32[]{:T(128)} %constant.277.clone.1..sunk.3, s32[]{:T(128)} %constant.277.clone.1..sunk.3) | dynamic-update-slice | bytes 1572868 | tf_op jit(solution)/shard_map/transpose(jvp())/while/body/jit(dynamic_update_index_in_dim)/dynamic_update_slice | solution.py:139
  616.3 9.5 fusion.254
  637.9 3.2 convolution_bitcast_fusion.4
  644.5 4.0 fusion.262
  649.3 16.7 %dynamic_update_slice.275 = f32[2,256,12,64]{1,0,3,2:T(2,128)} dynamic-update-slice(f32[2,256,12,64]{1,0,3,2:T(2,128)} %get-tuple-element.2665, f32[1,256,12,64]{1,0,3,2:T(1,128)S(1)} %copy.348, s32[]{:T(128)S(6)} %sub.279, s32[]{:T(128)} %constant.277.clone.1..sunk.3, s32[]{:T(128)} %constant.277.clone.1..sunk.3, s32[]{:T(128)} %constant.277.clone.1..sunk.3) | dynamic-update-slice | bytes 1572868 | tf_op jit(solution)/shard_map/transpose(jvp())/while/body/jit(dynamic_update_index_in_dim)/dynamic_update_slice | solution.py:139
  684.0 3.1 copy.255
  687.1 6.1 multiply_reduce_fusion.3
  698.6 3.7 all_to_all.106
  711.1 4.2 all_to_all.107
  720.4 5.2 all_to_all.108
  733.0 6.8 fusion.156
  739.9 54.5 %all-reduce.29.cloned.1.call-done = (f32[768,3352]{0,1:T(8,128)}, f32[1536,768]{1,0:T(8,128)}) async-done(((f32[768,3352]{0,1:T(8,128)}, f32[1536,768]{1,0:T(8,128)}), (f32[768,3352]{0,1:T(8,128)}, f32[1536,768]{1,0:T(8,128)})) %all-reduce.29.cloned.1.call-update) | async-done | bytes 15015952 | tf_op jit(solution)/shard_map/psum | solution.py:367
  795.2 3.2 fusion.138
  800.3 5.6 fusion.148
  805.9 3.7 all-reduce.22
  809.6 82.6 %all-reduce.20 = (f32[768]{0:T(1024)}, f32[4,1792]{1,0:T(4,128)}, f32[1792]{0:T(1024)}, f32[24]{0:T(128)}, f32[24]{0:T(128)}, /*index=5*/f32[24]{0:T(128)}, f32[1536]{0:T(1024)}) all-reduce(f32[768]{0:T(1024)S(1)} %get-tuple-element.1963, f32[4,1792]{1,0:T(4,128)S(1)} %get-tuple-element.1964, ...), channel_id=1, replica_groups=mesh['seq'=16,'head'=2] {'seq'}, use_global_device_ids=true, to_apply=%region_30.31 | all-reduce | flops 11336 | bytes 90688 | tf_op jit(solution)/shard_map/psum | solution.py:366
  894.5 326.4 %all-reduce.27.cloned.1.call-done = (f32[768,3352]{0,1:T(8,128)}, f32[1536,768]{1,0:T(8,128)}) async-done(((f32[768,3352]{0,1:T(8,128)}, f32[1536,768]{1,0:T(8,128)}), (f32[768,3352]{0,1:T(8,128)}, f32[1536,768]{1,0:T(8,128)})) %all-reduce.27.cloned.1.call-update) | async-done | bytes 15015952 | tf_op jit(solution)/shard_map/psum | solution.py:366
  1220.9 8.8 copy.485
  (726 shorter events, 227.5 us)
Async XLA Ops:
  7.2 326.1 %copy-start = (bf16[1536,768]{1,0:T(8,128)(2,1)S(1)}, bf16[1536,768]{1,0:T(8,128)(2,1)}, u32[]{:S(2)}) copy-start(bf16[1536,768]{1,0:T(8,128)(2,1)} %param.31) | copy-start | bytes 7077892
  14.6 12.8 %slice-start = ((bf16[256,3352]{0,1:T(8,128)(2,1)}), bf16[256,256]{0,1:T(8,128)(2,1)S(1)}, s32[]{:S(2)}) async-start(bf16[256,3352]{0,1:T(8,128)(2,1)} %copy-done.40), calls=%async_computation.12 | async-start | bytes 262144 | tf_op jit(solution)/shard_map/slice | solution.py:200
  15.8 16.0 %slice-start.1 = ((bf16[256,3352]{0,1:T(8,128)(2,1)}), bf16[256,24]{0,1:T(8,128)(2,1)S(1)}, s32[]{:S(2)}) async-start(bf16[256,3352]{0,1:T(8,128)(2,1)} %copy-done.40), calls=%async_computation.13 | async-start | bytes 24576 | tf_op jit(solution)/shard_map/slice | solution.py:202
  15.8 25.3 %copy-start.149 = (s32[2]{0:T(128)S(1)}, s32[2]{0:T(128)}, u32[]{:S(2)}) copy-start(s32[2]{0:T(128)} %param.22) | copy-start | bytes 28
  21.4 31.6 %copy-start.28 = (bf16[256,2,768]{2,0,1:T(8,128)(2,1)}, bf16[256,2,768]{2,0,1:T(8,128)(2,1)S(1)}, u32[]{:S(2)}) copy-start(bf16[256,2,768]{2,0,1:T(8,128)(2,1)S(1)} %all_to_all.103) | copy-start | bytes 2359300
  22.0 36.4 %collective-permute-start = (bf16[3,768]{1,0:T(4,128)(2,1)}, bf16[3,768]{1,0:T(4,128)(2,1)}, u32[]{:S(2)}, u32[]{:S(2)}) collective-permute-start(bf16[3,768]{1,0:T(4,128)(2,1)} %slice.198), channel_id=1, source_target_pairs={{0,4},{2,6},{4,8},{6,10},{8,12},{10,14},{12,16},{14,18},{16,20},{1... | collective-permute-start | bytes 13832 | tf_op jit(solution)/shard_map/ppermute | solution.py:21
  28.3 5.0 all-to-all-start.2
  33.3 19.7 %copy-start.46 = (bf16[256,2,256]{2,0,1:T(8,128)(2,1)}, bf16[256,2,256]{2,0,1:T(8,128)(2,1)S(1)}, u32[]{:S(2)}) copy-start(bf16[256,2,256]{2,0,1:T(8,128)(2,1)S(1)} %all-to-all-done.2) | copy-start | bytes 786436
  33.3 8.5 all-to-all-start
  36.5 184.3 %all-gather.3.cloned.1.call-start = ((), (), s32[]{:S(2)}) async-start(), calls=%async_computation.8 | async-start | bytes 13369344 | tf_op jit(solution)/shard_map/all_gather | solution.py:28
  37.2 17.7 %collective-permute-start.1 = (bf16[3,256]{1,0:T(4,128)(2,1)}, bf16[3,256]{1,0:T(4,128)(2,1)}, u32[]{:S(2)}, u32[]{:S(2)}) collective-permute-start(bf16[3,256]{1,0:T(4,128)(2,1)} %slice.204), channel_id=1, source_target_pairs={{0,4},{2,6},{4,8},{6,10},{8,12},{10,14},{12,16},{14,18},{16,20},{1... | collective-permute-start | bytes 4616 | tf_op jit(solution)/shard_map/ppermute | solution.py:21
  41.7 69.1 %copy-start.77 = (bf16[256,2,12]{0,2,1:T(8,128)(2,1)}, bf16[256,2,12]{0,2,1:T(8,128)(2,1)S(1)}, u32[]{:S(2)}) copy-start(bf16[256,2,12]{0,2,1:T(8,128)(2,1)S(1)} %all-to-all-done) | copy-start | bytes 36868
  41.7 11.2 copy-start.71
  42.5 16.7 %copy-start.91 = (f32[512]{0:T(512)}, f32[512]{0:T(512)S(1)}, u32[]{:S(2)}) copy-start(f32[512]{0:T(512)S(1)} %fusion.181) | copy-start | bytes 6148
  43.2 9.7 copy-start.121
  54.9 6.9 copy-start.103
  54.9 6.9 copy-start.105
  54.9 6.9 copy-start.107
  54.9 6.9 copy-start.109
  58.4 53.2 %copy-start.35 = (f32[512,256]{1,0:T(8,128)}, f32[512,256]{1,0:T(8,128)S(1)}, u32[]{:S(2)}) copy-start(f32[512,256]{1,0:T(8,128)S(1)} %get-tuple-element.1985) | copy-start | bytes 1572868
  67.8 39.9 %copy-start.147 = (f32[24]{0:T(128)S(1)}, f32[24]{0:T(128)}, u32[]{:S(2)}) copy-start(f32[24]{0:T(128)} %param.28) | copy-start | bytes 292
  67.8 43.1 %copy-start.122 = (f32[12]{0:T(128)S(1)}, f32[12]{0:T(128)}, u32[]{:S(2)}) copy-start(f32[12]{0:T(128)} %copy-done.121) | copy-start | bytes 148
  68.9 460.7 %all-gather.5.cloned.1.call-start = ((), (), s32[]{:S(2)}) async-start(), calls=%async_computation.9 | async-start | bytes 13369344 | tf_op jit(solution)/shard_map/all_gather | solution.py:28
  333.3 87.9 %copy-start.98 = (f32[256]{0:T(256)}, f32[256]{0:T(256)S(1)}, u32[]{:S(2)}) copy-start(f32[256]{0:T(256)S(1)} %get-tuple-element.2023) | copy-start | bytes 3076
  358.9 435.5 %all-reduce.29.cloned.1.call-start = ((), (), s32[]{:S(2)}) async-start(), calls=%async_computation.11 | async-start | bytes 30031872 | tf_op jit(solution)/shard_map/psum | solution.py:367
  555.8 9.5 copy-start.1
  555.8 9.5 copy-start.21
  555.8 10.2 copy-start.11
  576.1 8.0 copy-start.70
  576.1 8.0 copy-start.2
  605.7 8.3 copy-start.51
  605.7 8.3 copy-start.63
  605.7 8.3 copy-start.73
  616.3 9.5 copy-start.1
  616.3 9.5 copy-start.21
  616.3 10.2 copy-start.11
  636.6 7.9 copy-start.70
  636.6 7.9 copy-start.2
  666.1 8.3 copy-start.51
  666.1 8.3 copy-start.63
  666.1 8.3 copy-start.73
  680.0 29.8 %collective-permute-start.3 = (f32[3,256]{1,0:T(4,128)}, f32[3,256]{1,0:T(4,128)}, u32[]{:S(2)}, u32[]{:S(2)}) collective-permute-start(f32[3,256]{1,0:T(4,128)} %add_multiply_fusion.1), channel_id=1, source_target_pairs={{4,0},{6,2},{8,4},{10,6},{12,8},{14,10},{16,12},{18,14},{20,16},{2... | collective-permute-start | bytes 9224 | tf_op jit(solution)/shard_map/ppermute | solution.py:21
  698.6 7.7 copy-start.126
  706.3 9.8 collective-permute-start.2
  739.8 481.1 %all-reduce.27.cloned.1.call-start = ((), (), s32[]{:S(2)}) async-start(), calls=%async_computation.10 | async-start | bytes 30031872 | tf_op jit(solution)/shard_map/psum | solution.py:366
  800.3 91.9 %copy-start.43 = (bf16[256,768]{1,0:T(8,128)(2,1)S(1)}, bf16[256,768]{1,0:T(8,128)(2,1)}, u32[]{:S(2)}) copy-start(bf16[256,768]{1,0:T(8,128)(2,1)} %param.21) | copy-start | bytes 1179652
  800.3 91.9 %copy-start.135 = (f32[256]{0:T(256)S(1)}, f32[256]{0:T(256)}, u32[]{:S(2)}) copy-start(f32[256]{0:T(256)} %get-tuple-element.2020) | copy-start | bytes 3076
  1220.9 8.8 copy-start.34
  (164 other events, 554.4 us)
Sparse Core Ops, SparseCore 0:
  69.0 151.7 all-gather.2
  359.0 170.5 all-gather.4
  740.0 54.3 all-reduce.28
  801.8 419.1 all-reduce.26
